TPU v7x, 128 devices: a whole 4x4x4 slice. The times are simulated.
128 devices in a mesh: ep: 8 (over z, core), dp: 16 (over y, x).
Axes of the slice: x: 4, y: 4, z: 4, core: 2. Of those that a mesh axis runs over, the one named last changes fastest.
Arguments:
- tokens: bfloat16 [32768, 1024], P(('ep', 'dp')), may hold values from -6 to 6
- lengths: int32 [8, 2], P('ep'), may hold values from 1 to 3072, 4096 in all within a row
- adapter_ids: int32 [8, 2], replicated, may hold values from 0 to 63
- expert_ids: int32 [32768, 8], P(('ep', 'dp')), may hold values from 0 to 31, all different within a row; in each aligned block of 256 rows (0 to 255, 256 to 511, ...) at most 96 rows name the same one
- attn_gain: bfloat16 [1024], replicated, may hold values from 0.5 to 1.5
- w_qkv: bfloat16 [1024, 2048], replicated, may hold values from -3 to 3
- w_out: bfloat16 [1024, 1024], replicated, may hold values from -0.1875 to 0.1875
- moe_gain: bfloat16 [1024], replicated, may hold values from 0.5 to 1.5
- w_router: bfloat16 [1024, 32], replicated, may hold values from -12 to 12
- w_gate_up: bfloat16 [32, 1024, 1024], P('ep'), may hold values from -0.1875 to 0.1875
- w_down: bfloat16 [32, 512, 1024], P('ep'), may hold values from -0.25 to 0.25
- adapter_in: bfloat16 [64, 1024, 64], P('dp'), may hold values from -0.1875 to 0.1875
- adapter_out: bfloat16 [64, 16, 4096], P('dp'), may hold values from -0.75 to 0.75
- adapter_expert: bfloat16 [64, 48, 512], P('dp'), may hold values from -0.75 to 0.75
Outputs:
- layer_out: bfloat16 [32768, 1024], P(('ep', 'dp'))
Inputs may be any that keep to these rules, and one draw needn't show every extreme that they name: `lengths`: each row sums to 4096. `expert_ids`: each row names 8 different experts; among the 256 rows of one device no expert is named more than 96 times.
All inputs are finite; a program needn't handle non-finite values.
Results may differ from a plain program's by a relative error of at most 0.02.
The roundings to bfloat16 on the way count: a program that leaves them out, or rounds other values in their place, can miss the bound.
Values may be sent and summed in bfloat16 or wider, within the bound.
A program may use at most 256 MiB of HBM per device.

v0:
```python
import math
import jax
import jax.numpy as jnp
from jax import lax
from jax.sharding import PartitionSpec as P

HEADS = 16
KV_HEADS = 8
HEAD = 64
CAP = 96
EPS = 1e-06
THETA = 10000.0
NEG_BIG = -1e30


def rms_norm(values_in, gain_vec):
    floats = values_in.astype(jnp.float32)
    meansq = jnp.mean(floats * floats, axis=-1, keepdims=True)
    return (floats * lax.rsqrt(meansq + EPS) * gain_vec.astype(jnp.float32)).astype(jnp.bfloat16)


def rotate(vectors, position):
    half_dim = vectors.shape[-1] // 2
    frequency = THETA ** (-jnp.arange(half_dim, dtype=jnp.float32) / half_dim)
    angles = position.astype(jnp.float32)[:, None] * frequency[None, :]
    cosine = jnp.cos(angles)[:, None, :]
    sine_val = jnp.sin(angles)[:, None, :]
    first_half = vectors[..., :half_dim]
    second_half = vectors[..., half_dim:]
    return jnp.concatenate(
        [
            first_half * cosine - second_half * sine_val,
            second_half * cosine + first_half * sine_val,
        ],
        axis=-1,
    )


def request_layout(lengths_row, first_pos, row_count):
    position = first_pos + jnp.arange(row_count, dtype=jnp.int32)
    req_ends = jnp.cumsum(lengths_row)
    starts = req_ends - lengths_row
    request = jnp.sum((position[:, None] >= req_ends[None, :]).astype(jnp.int32), axis=1)
    slot_hot = request[:, None] == jnp.arange(lengths_row.shape[0], dtype=jnp.int32)[None, :]
    req_start = jnp.sum(jnp.where(slot_hot, starts[None, :], 0), axis=1)
    return (position, req_start, slot_hot)


def low_rank(inputs, a_sel, slot_hot):
    count_r = a_sel.shape[2]
    a_cat = jnp.transpose(a_sel, (1, 0, 2)).reshape(inputs.shape[1], -1)
    coeffs = jnp.dot(inputs, a_cat, preferred_element_type=jnp.float32)
    keep_mask = jnp.repeat(slot_hot, count_r, axis=1)
    return jnp.where(keep_mask, coeffs, 0.0).astype(jnp.bfloat16)


def earlier_counts(flat_ids, n_experts):
    expert_hot = (flat_ids[:, None] == jnp.arange(n_experts, dtype=jnp.int32)[None, :]).astype(
        jnp.int32
    )
    return jnp.sum((jnp.cumsum(expert_hot, axis=0) - expert_hot) * expert_hot, axis=1)


def per_device(
    tokens,
    lengths,
    adapter_ids,
    expert_ids,
    attn_gain,
    w_qkv,
    w_out,
    moe_gain,
    w_router,
    w_gate_up,
    w_down,
    adapter_in,
    adapter_out,
    adapter_expert,
):
    n_ep = lax.axis_size("ep")
    group_idx = lax.axis_index("ep")
    row_idx = lax.axis_index("dp")
    tok_count = tokens.shape[0]
    model_width = tokens.shape[1]
    rank_r = adapter_in.shape[2] // 4
    q_width = HEADS * HEAD
    kv_width = KV_HEADS * HEAD
    qkv_width = q_width + 2 * kv_width
    group_ratio = HEADS // KV_HEADS
    ff_width = w_down.shape[1]
    exp_local = w_gate_up.shape[0]
    n_requests = lengths.shape[1]
    top_count = expert_ids.shape[1]
    position, req_start, slot_hot = request_layout(lengths[0], row_idx * tok_count, tok_count)
    group_ids = lax.dynamic_index_in_dim(adapter_ids, group_idx, 0, keepdims=False)
    all_in, all_out, all_expert = (
        lax.all_gather(adapter_in, "dp", axis=0, tiled=True),
        lax.all_gather(adapter_out, "dp", axis=0, tiled=True),
        lax.all_gather(adapter_expert, "dp", axis=0, tiled=True),
    )
    sel_in = jnp.take(all_in, group_ids, axis=0)
    sel_out = jnp.take(all_out, group_ids, axis=0)
    normed = rms_norm(tokens, attn_gain)
    z_qkv = low_rank(normed, sel_in[:, :, 0:rank_r], slot_hot)
    projected = jnp.dot(normed, w_qkv, preferred_element_type=jnp.float32)
    projected = projected + jnp.dot(
        z_qkv, sel_out[:, :, 0:qkv_width].reshape(-1, qkv_width), preferred_element_type=jnp.float32
    )
    rel_pos = position - req_start
    queries = rotate(projected[:, :q_width].reshape(tok_count, HEADS, HEAD), rel_pos).astype(
        jnp.bfloat16
    )
    keys_rot = rotate(
        projected[:, q_width : q_width + kv_width].reshape(tok_count, KV_HEADS, HEAD), rel_pos
    ).astype(jnp.bfloat16)
    keys_rot = keys_rot.reshape(tok_count, kv_width)
    values_v = projected[:, q_width + kv_width :].astype(jnp.bfloat16)
    query_grp = queries.reshape(tok_count, KV_HEADS, group_ratio, HEAD)
    score_scale = 1.0 / math.sqrt(HEAD)
    last_pos = position[tok_count - 1]
    first_start = req_start[0]
    init_state = (
        jnp.full((tok_count, KV_HEADS, group_ratio), NEG_BIG, jnp.float32),
        jnp.zeros((tok_count, KV_HEADS, group_ratio), jnp.float32),
        jnp.zeros((tok_count, KV_HEADS, group_ratio, HEAD), jnp.float32),
    )
    first_row = jnp.int32(0)
    keys_in = lax.all_gather(keys_rot, "dp", axis=0, tiled=True)
    vals_in = lax.all_gather(values_v, "dp", axis=0, tiled=True)
    rows_in = keys_in.shape[0]
    key_pos = jnp.arange(rows_in, dtype=jnp.int32)

    def compute(state):
        run_max, run_sum, run_acc = state
        scores = (
            jnp.einsum(
                "tgrd,sgd->tgrs",
                query_grp,
                keys_in.reshape(rows_in, KV_HEADS, HEAD),
                preferred_element_type=jnp.float32,
            )
            * score_scale
        )
        allowed = (key_pos[None, :] >= req_start[:, None]) & (key_pos[None, :] <= position[:, None])
        allowed = allowed[:, None, None, :]
        scores = jnp.where(allowed, scores, NEG_BIG)
        new_max = jnp.maximum(run_max, jnp.max(scores, axis=-1))
        weights = jnp.where(allowed, jnp.exp(scores - new_max[..., None]), 0.0)
        new_sum = jnp.sum(weights, axis=-1)
        mixed_vals = jnp.einsum(
            "tgrs,sgd->tgrd",
            weights.astype(jnp.bfloat16),
            vals_in.reshape(rows_in, KV_HEADS, HEAD),
            preferred_element_type=jnp.float32,
        )
        return (new_max, new_sum, mixed_vals)

    relevant = (first_row <= last_pos) & (first_row + rows_in - 1 >= first_start)
    run_max, run_sum, run_acc = lax.cond(relevant, compute, lambda state: state, init_state)
    attended = (run_acc / run_sum[..., None]).reshape(tok_count, q_width).astype(jnp.bfloat16)
    z_out = low_rank(attended, sel_in[:, :, rank_r : 2 * rank_r], slot_hot)
    residual = tokens.astype(jnp.float32) + jnp.dot(
        attended, w_out, preferred_element_type=jnp.float32
    )
    residual = residual + jnp.dot(
        z_out,
        sel_out[:, :, qkv_width : qkv_width + model_width].reshape(-1, model_width),
        preferred_element_type=jnp.float32,
    )
    residual = residual.astype(jnp.bfloat16)
    normed_two = rms_norm(residual, moe_gain)
    logits = jnp.dot(normed_two, w_router, preferred_element_type=jnp.float32)
    gate_weights = jax.nn.softmax(jnp.take_along_axis(logits, expert_ids, axis=1), axis=1)
    z_experts = low_rank(normed_two, sel_in[:, :, 2 * rank_r : 4 * rank_r], slot_hot)
    z_width = z_experts.shape[1]
    n_experts = exp_local * n_ep
    chosen = jnp.take(all_expert, adapter_ids.reshape(-1), axis=0).reshape(
        n_ep, n_requests, 3 * rank_r, ff_width
    )
    b_gate = chosen[:, :, 0:rank_r]
    b_up = chosen[:, :, rank_r : 2 * rank_r]
    blank_blk = jnp.zeros_like(b_gate)
    b_joint = jnp.concatenate(
        [jnp.concatenate([b_gate, blank_blk], axis=3), jnp.concatenate([blank_blk, b_up], axis=3)],
        axis=2,
    )
    b_joint = b_joint.reshape(n_ep, n_requests * 2 * rank_r, 2 * ff_width)
    a_down = jnp.transpose(chosen[:, :, 2 * rank_r : 3 * rank_r], (0, 3, 1, 2)).reshape(
        n_ep, ff_width, n_requests * rank_r
    )
    keep_mask = jnp.repeat(slot_hot, rank_r, axis=1)
    flat_expert = expert_ids.reshape(-1)
    earlier = earlier_counts(flat_expert, n_experts)
    slot_dest = flat_expert * CAP + earlier
    source_row = (
        jnp.full((n_experts * CAP,), tok_count, jnp.int32)
        .at[slot_dest]
        .set(jnp.arange(tok_count * top_count, dtype=jnp.int32) // top_count)
    )
    padded_x = jnp.concatenate([normed_two, jnp.zeros((1, model_width), jnp.bfloat16)])
    padded_z = jnp.concatenate([z_experts, jnp.zeros((1, z_width), jnp.bfloat16)])
    send_x = padded_x[source_row].reshape(n_ep, exp_local, CAP, model_width)
    send_z = padded_z[source_row].reshape(n_ep, exp_local, CAP, z_width)
    recv_x, recv_z = (
        lax.all_to_all(send_x, "ep", split_axis=0, concat_axis=0, tiled=True),
        lax.all_to_all(send_z, "ep", split_axis=0, concat_axis=0, tiled=True),
    )
    pre_act = jnp.einsum("jecd,edf->jecf", recv_x, w_gate_up, preferred_element_type=jnp.float32)
    pre_act = pre_act + jnp.einsum(
        "jecr,jrf->jecf", recv_z, b_joint, preferred_element_type=jnp.float32
    )
    hidden = (jax.nn.silu(pre_act[..., :ff_width]) * pre_act[..., ff_width:]).astype(jnp.bfloat16)
    expert_out = jnp.einsum(
        "jech,ehd->jecd", hidden, w_down, preferred_element_type=jnp.float32
    ).astype(jnp.bfloat16)
    down_coeff = jnp.einsum(
        "jech,jhr->jecr", hidden, a_down, preferred_element_type=jnp.float32
    ).astype(jnp.bfloat16)
    expert_out, down_coeff = (expert_out, down_coeff)
    back_out, back_coeff = (
        lax.all_to_all(expert_out, "ep", split_axis=0, concat_axis=0, tiled=True),
        lax.all_to_all(down_coeff, "ep", split_axis=0, concat_axis=0, tiled=True),
    )
    rows_out = back_out.reshape(n_experts * CAP, model_width)[slot_dest].reshape(
        tok_count, top_count, model_width
    )
    rows_coeff = back_coeff.reshape(n_experts * CAP, -1)[slot_dest].reshape(
        tok_count, top_count, -1
    )
    owner_hot = (expert_ids // exp_local)[:, :, None] == jnp.arange(n_ep, dtype=jnp.int32)[
        None, None, :
    ]
    weighted = jnp.where(owner_hot, gate_weights[:, :, None], 0.0)
    part_out = jnp.einsum(
        "tkg,tkd->tgd", weighted, rows_out.astype(jnp.float32), precision=lax.Precision.HIGHEST
    ).astype(jnp.bfloat16)
    part_coeff = jnp.einsum(
        "tkg,tkr->tgr", weighted, rows_coeff.astype(jnp.float32), precision=lax.Precision.HIGHEST
    ).astype(jnp.bfloat16)
    moe_sum = jnp.sum(part_out.astype(jnp.float32), axis=1)
    coeff_sum = jnp.sum(
        jnp.where(keep_mask[:, None, :], part_coeff.astype(jnp.float32), 0.0), axis=1
    ).astype(jnp.bfloat16)
    down_delta = jnp.dot(
        coeff_sum,
        sel_out[:, :, qkv_width + model_width : qkv_width + 2 * model_width].reshape(
            -1, model_width
        ),
        preferred_element_type=jnp.float32,
    )
    return (residual.astype(jnp.float32) + moe_sum + down_delta).astype(jnp.bfloat16)


def solution(mesh):
    return jax.shard_map(
        per_device,
        mesh=mesh,
        in_specs=(
            P(("ep", "dp"), None),
            P("ep", None),
            P(),
            P(("ep", "dp"), None),
            P(),
            P(),
            P(),
            P(),
            P(),
            P("ep", None, None),
            P("ep", None, None),
            P("dp", None, None),
            P("dp", None, None),
            P("dp", None, None),
        ),
        out_specs=P(("ep", "dp"), None),
        check_vma=False,
    )
```

profile of v0, /device:TPU:1, one launch (start us, length us, event | category | flops | bytes accessed | tf_op | source)
XLA Modules:
  0.0 616.2 jit_solution(15493466018963444724)
XLA Ops:
  12.8 5.0 fusion.72
  17.9 65.3 %all-gather.8.cloned.1.call-done = bf16[64,16,4096]{2,1,0:T(8,128)(2,1)} async-done(((bf16[4,16,4096]{2,1,0:T(8,128)(2,1)}), bf16[64,16,4096]{2,1,0:T(8,128)(2,1)}) %all-gather.8.cloned.1.call-update) | async-done | bytes 8388624 | tf_op jit(solution)/shard_map/all_gather | solution.py:98
  83.2 3.9 gather_fusion.1
  88.0 67.7 %all-gather.6.cloned.1.call-done = bf16[64,1024,64]{1,2,0:T(8,128)(2,1)} async-done(((bf16[4,1024,64]{1,2,0:T(8,128)(2,1)}), bf16[64,1024,64]{1,2,0:T(8,128)(2,1)}) %all-gather.6.cloned.1.call-update) | async-done | bytes 8388624 | tf_op jit(solution)/shard_map/all_gather | solution.py:97
  155.8 3.9 gather_fusion
  160.6 4.0 convolution_add_fusion
  164.6 2.0 slice.107
  166.5 2.0 copy.115
  170.4 1.8 slice.138
  179.1 15.9 %reduce-window.11 = s32[32,16,128]{2,1,0:T(8,128)S(1)} reduce-window(s32[32,16,128]{2,1,0:T(8,128)} %fusion.69, s32[]{:T(128)} %constant.130.clone.1), window={size=1x1x128 pad=0_0x0_0x127_0}, to_apply=%region_11.12 | reduce-window | flops 8323072 | bytes 524292 | tf_op jit(solution)/shard_map/reduce-window.1
  195.9 1.8 copy.147
  197.7 1.5 reduce-window.14
  200.9 8.2 %scatter_custom_fusion = s32[3072]{0:T(1024)S(1)} fusion(s32[2048]{0:T(1024)S(1)} %bitcast.173, s32[2048]{0:T(1024)} %add_select_fusion, s32[]{:T(128)} %constant.128.clone.1), kind=kCustom, calls=%fused_computation.129 | custom fusion | bytes 12800 | tf_op jit(solution)/shard_map/scatter | solution.py:198
  209.2 1.5 fusion.98
  210.7 1.4 copy.116
  212.1 1.4 subtract_convert_fusion
  213.5 12.3 %all-gather.10.cloned.1.call-done = bf16[4096,512]{0,1:T(8,128)(2,1)} async-done(((bf16[256,512]{0,1:T(8,128)(2,1)}), bf16[4096,512]{0,1:T(8,128)(2,1)}) %all-gather.10.cloned.1.call-update) | async-done | bytes 4194320 | tf_op jit(solution)/shard_map/all_gather | solution.py:128
  225.8 53.9 %all-gather.12.cloned.1.call-done = bf16[4096,512]{1,0:T(8,128)(2,1)} async-done(((bf16[256,512]{1,0:T(8,128)(2,1)}), bf16[4096,512]{1,0:T(8,128)(2,1)}) %all-gather.12.cloned.1.call-update) | async-done | bytes 4194320 | tf_op jit(solution)/shard_map/all_gather | solution.py:129
  279.7 88.2 %conditional.1 = (f32[256,8,2]{0,2,1:T(2,128)S(1)}, f32[256,8,2,64]{0,3,2,1:T(8,128)}) conditional(s32[]{:T(128)} %bitcast.12, () %tuple.13, (s32[4096]{0:T(1024)S(1)}, s32[4096]{0:T(1024)S(1)}, s32[256]{0:T(256)S(1)}, s32[256]{0:T(256)S(1)}, bf16[4096,512]{0,1:T(8,128)(2,1)}, /*index=5*/bf16[256,8,2,64]{0,3,2,1:T(8,128)(2,1)S(1)}, ...), branch_computations={%region_4.5_spmd, %region_5.8_spmd} | conditional | flops 4516212736 | bytes 224004112 | solution.py:159
  280.2 3.9 compare_and_fusion
  284.0 26.5 %fusion = (f32[256,8,2]{0,2,1:T(2,128)S(1)}, f32[8,4096,256,2]{2,1,3,0:T(8,128)}) fusion(pred[256,4096]{0,1:T(8,128)(4,1)} %compare_and_fusion, bf16[4096,8,64,1]{0,2,3,1:T(8,128)(2,1)} %bitcast.176, bf16[256,8,2,64]{0,3,2,1:T(8,128)(2,1)S(1)} %get-tuple-element.23), kind=kOutput, calls=%fused_computation.11 | convolution fusion | flops 2197811200 | bytes 72892416 | tf_op jit(solution)/shard_map/cond/branch_1_fun/tgrd,sgd->tgrs/dot_general | solution.py:136
  310.5 22.8 %fusion.2 = f32[256,8,2]{0,2,1:T(2,128)S(1)} fusion(f32[8,4096,256,2]{2,1,3,0:T(8,128)} %get-tuple-element.65, f32[256,8,2]{0,2,1:T(2,128)S(1)} %broadcast_maximum_fusion, pred[256,4096]{0,1:T(8,128)(4,1)} %compare_and_fusion), kind=kLoop, calls=%fused_computation.13 | loop fusion | flops 83881984 | bytes 68190208 | tf_op jit(solution)/shard_map/cond/branch_1_fun/reduce_sum | solution.py:149
  333.3 6.4 %copy.117 = bf16[4096,512]{0,1:T(8,128)(2,1)} copy(bf16[4096,512]{1,0:T(8,128)(2,1)} %get-tuple-element.63) | data formatting | bytes 8388608 | tf_op jit(solution)/shard_map
  339.7 28.1 %fusion.6 = f32[256,8,2,64]{0,3,2,1:T(8,128)} fusion(bf16[4096,8,64,1]{0,2,3,1:T(8,128)(2,1)} %bitcast.150, f32[8,4096,256,2]{2,1,3,0:T(8,128)} %get-tuple-element.65, f32[256,8,2]{0,2,1:T(2,128)S(1)} %broadcast_maximum_fusion, pred[256,4096]{0,1:T(8,128)(4,1)} %compare_and_fusion), kind=kOutput, calls=%fused_computation.17 | convolution fusion | flops 2231369728 | bytes 73416704 | tf_op jit(solution)/shard_map/cond/branch_1_fun/tgrs,sgd->tgrd/dot_general | solution.py:150
  367.8 1.3 divide_convert_fusion
  369.2 1.7 convert_add_fusion.1
  370.9 1.9 fusion.54
  373.1 14.0 %gather_fusion.2 = bf16[3072,1024]{1,0:T(8,128)(2,1)} fusion(bf16[257,1024]{1,0:T(8,128)(2,1)S(1)} %concatenate.32, s32[3072]{0:T(1024)S(1)} %fusion.77), kind=kCustom, calls=%fused_computation.2 | custom fusion | bytes 12595200 | tf_op jit(solution)/shard_map/gather | solution.py:202
  387.1 5.8 all-to-all-start
  393.3 2.5 gather_fusion.4
  397.6 9.2 %gather_fusion.3 = bf16[3072,64]{1,0:T(8,128)(2,1)S(1)} fusion(bf16[257,64]{1,0:T(8,128)(2,1)S(1)} %concatenate.33.clone, s32[3072]{0:T(1024)S(1)} %copy-done.11), kind=kCustom, calls=%fused_computation.3 | custom fusion | bytes 798720 | tf_op jit(solution)/shard_map/gather | solution.py:203
  407.9 56.4 %all-to-all-done = bf16[8,4,96,1024]{3,2,1,0:T(8,128)(2,1)} async-done(((bf16[8,4,96,1024]{3,2,1,0:T(8,128)(2,1)}), bf16[8,4,96,1024]{3,2,1,0:T(8,128)(2,1)}, u32[]{:S(2)}, u32[]{:S(2)}) %all-to-all-start) | async-done | bytes 6291488 | tf_op jit(solution)/shard_map/all_to_all | solution.py:205
  464.2 4.4 all-to-all-start.1
  468.6 13.8 %fusion.12 = f32[4,8,96,1024]{3,2,1,0:T(8,128)} fusion(bf16[4,1024,1024]{2,1,0:T(8,128)(2,1)} %param.25, bf16[8,4,96,1024]{3,2,1,0:T(8,128)(2,1)} %all-to-all-done), kind=kOutput, calls=%fused_computation.23 | convolution fusion | flops 6442450944 | bytes 27262976 | tf_op jit(solution)/shard_map/jecd,edf->jecf/dot_general | solution.py:208
  482.4 6.7 %bitcast_add_fusion = f32[8,4,96,1024]{3,2,0,1:T(8,128)S(1)} fusion(f32[4,8,96,1024]{3,2,1,0:T(8,128)} %fusion.12, bf16[8,64,1024,1]{2,1,0,3:T(8,128)(2,1)} %bitcast.149, bf16[8,4,96,64]{2,3,1,0:T(8,128)(2,1)S(1)} %all-to-all-done.1), kind=kOutput, calls=%fused_computation.22 | convolution fusion | flops 405798912 | bytes 26607616 | tf_op jit(solution)/shard_map/jecr,jrf->jecf/dot_general | solution.py:209
  489.2 2.1 fusion.14
  491.2 1.6 copy-done.4
  492.9 1.9 fusion.45
  494.8 4.8 all-to-all-start.3
  499.6 6.6 %convert_bitcast_fusion = bf16[8,4,96,1024]{3,2,0,1:T(8,128)(2,1)S(1)} fusion(bf16[8,4,96,512]{3,2,0,1:T(8,128)(2,1)} %copy-done.4, bf16[4,512,1024]{2,1,0:T(8,128)(2,1)} %param.26), kind=kOutput, calls=%fused_computation.29 | convolution fusion | flops 3224371200 | bytes 13631488 | tf_op jit(solution)/shard_map/jech,ehd->jecd/dot_general | solution.py:213
  506.2 3.3 copy.134
  509.6 5.2 all-to-all-start.2
  515.6 16.8 %gather_fusion.7 = f32[2048]{0:T(1024)S(1)} fusion(f32[256,32]{0,1:T(8,128)S(1)} %fusion.99, s32[2048]{0:T(1024)S(1)} %reshape.451), kind=kCustom, calls=%fused_computation.7 | custom fusion | bytes 32768 | tf_op jit(solution)/shard_map/jit(take_along_axis)/gather | solution.py:173
  533.1 6.2 %gather_fusion.6 = bf16[2048,32]{1,0:T(8,128)(2,1)S(1)} fusion(bf16[3072,32]{1,0:T(8,128)(2,1)S(1)} %bitcast.145, s32[2048]{0:T(1024)S(1)} %broadcast_clamp_fusion), kind=kCustom, calls=%fused_computation.6 | custom fusion | bytes 270336 | tf_op jit(solution)/shard_map/gather | solution.py:227
  539.3 1.3 fusion.42
  540.6 45.3 %all-to-all-done.2 = bf16[8,4,96,1024]{3,2,1,0:T(8,128)(2,1)} async-done(((bf16[8,4,96,1024]{3,2,1,0:T(8,128)(2,1)}), bf16[8,4,96,1024]{3,2,1,0:T(8,128)(2,1)}, u32[]{:S(2)}, u32[]{:S(2)}) %all-to-all-start.2) | async-done | bytes 6291488 | tf_op jit(solution)/shard_map/all_to_all | solution.py:221
  586.0 14.8 %gather_fusion.5 = bf16[2048,1024]{1,0:T(8,128)(2,1)} fusion(bf16[3072,1024]{1,0:T(8,128)(2,1)} %bitcast.48, s32[2048]{0:T(1024)S(1)} %broadcast_clamp_fusion), kind=kCustom, calls=%fused_computation.5 | custom fusion | bytes 8396800 | tf_op jit(solution)/shard_map/gather | solution.py:224
  600.8 7.5 %convert_reduce_fusion = f32[256,1024]{1,0:T(8,128)S(1)} fusion(bf16[2048,1024]{1,0:T(8,128)(2,1)} %gather_fusion.5, f32[256,8]{1,0:T(8,128)S(1)} %copy.121, s32[256,8]{1,0:T(8,128)S(1)} %copy.118), kind=kOutput, calls=%fused_computation.25 | convolution fusion | flops 207388672 | bytes 5259264 | tf_op jit(solution)/shard_map/tkg,tkd->tgd/dot_general | solution.py:234
  (140 shorter events, 23.7 us)
Async XLA Ops:
  6.5 362.6 %copy-start = (bf16[1024,1024]{1,0:T(8,128)(2,1)S(1)}, bf16[1024,1024]{1,0:T(8,128)(2,1)}, u32[]{:S(2)}) copy-start(bf16[1024,1024]{1,0:T(8,128)(2,1)} %param.22) | copy-start | bytes 6291460
  6.5 154.0 %copy-start.2 = (bf16[256,1024]{1,0:T(8,128)(2,1)S(1)}, bf16[256,1024]{1,0:T(8,128)(2,1)}, u32[]{:S(2)}) copy-start(bf16[256,1024]{1,0:T(8,128)(2,1)} %param.16) | copy-start | bytes 1572868
  6.5 76.7 %all-gather.8.cloned.1.call-start = ((), (), s32[]{:S(2)}) async-start(), calls=%async_computation.5 | async-start | bytes 8912896 | tf_op jit(solution)/shard_map/all_gather | solution.py:98
  7.3 148.5 %all-gather.6.cloned.1.call-start = ((), (), s32[]{:S(2)}) async-start(), calls=%async_computation.4 | async-start | bytes 8912896 | tf_op jit(solution)/shard_map/all_gather | solution.py:97
  8.0 217.8 %all-gather.10.cloned.1.call-start = ((), (), s32[]{:S(2)}) async-start(), calls=%async_computation.6 | async-start | bytes 4456448 | tf_op jit(solution)/shard_map/all_gather | solution.py:128
  10.5 162.4 %copy-start.22 = (s32[256]{0:T(256)}, s32[256]{0:T(256)S(1)}, u32[]{:S(2)}) copy-start(s32[256]{0:T(256)S(1)} %iota_add_fusion) | copy-start | bytes 3076
  11.3 162.2 %copy-start.19 = (s32[256]{0:T(256)}, s32[256]{0:T(256)S(1)}, u32[]{:S(2)}) copy-start(s32[256]{0:T(256)S(1)} %select_reduce_fusion) | copy-start | bytes 3076
  12.6 152.0 %copy-start.17 = (pred[256,2]{0,1:T(4,128)(4,1)}, pred[256,2]{0,1:T(4,128)(4,1)S(1)}, u32[]{:S(2)}) copy-start(pred[256,2]{0,1:T(4,128)(4,1)S(1)} %iota_compare_fusion.7) | copy-start | bytes 1540
  17.9 156.2 %copy-start.7 = (s32[256,8]{0,1:T(8,128)S(1)}, s32[256,8]{0,1:T(8,128)}, u32[]{:S(2)}) copy-start(s32[256,8]{0,1:T(8,128)} %param.19) | copy-start | bytes 24580
  87.2 89.8 %copy-start.24 = (bf16[1024]{0:T(1024)(128)(2,1)S(1)}, bf16[1024]{0:T(1024)(128)(2,1)}, u32[]{:S(2)}) copy-start(bf16[1024]{0:T(1024)(128)(2,1)} %param.23) | copy-start | bytes 6148
  87.3 0.7 copy-start.6
  159.8 0.7 copy-start.5
  164.6 46.1 %slice-start = ((f32[256,2048]{1,0:T(8,128)}), f32[256,1024]{1,0:T(8,128)S(1)}, s32[]{:S(2)}) async-start(f32[256,2048]{1,0:T(8,128)} %convolution_add_fusion), calls=%async_computation.9 | async-start | bytes 2097152 | tf_op jit(solution)/shard_map/slice | solution.py:110
  170.4 109.3 %all-gather.12.cloned.1.call-start = ((), (), s32[]{:S(2)}) async-start(), calls=%async_computation.7 | async-start | bytes 4456448 | tf_op jit(solution)/shard_map/all_gather | solution.py:129
  172.3 221.1 %all-gather.14.cloned.1.call-start = ((), (), s32[]{:S(2)}) async-start(), calls=%async_computation.8 | async-start | bytes 3342336 | tf_op jit(solution)/shard_map/all_gather | solution.py:99
  200.0 79.6 %copy-start.20 = (s32[256]{0:T(256)S(1)}, s32[256]{0:T(256)}, u32[]{:S(2)}) copy-start(s32[256]{0:T(256)} %copy-done.19) | copy-start | bytes 3076
  200.1 79.6 %copy-start.23 = (s32[256]{0:T(256)S(1)}, s32[256]{0:T(256)}, u32[]{:S(2)}) copy-start(s32[256]{0:T(256)} %copy-done.22) | copy-start | bytes 3076
  200.9 8.2 %copy-start.14 = (s32[2048,1]{0,1:T(1,128)}, s32[2048,1]{0,1:T(1,128)S(1)}, u32[]{:S(2)}) copy-start(s32[2048,1]{0,1:T(1,128)S(1)} %compare_select_fusion) | copy-start | bytes 24580
  209.2 164.0 %copy-start.10 = (s32[3072]{0:T(1024)}, s32[3072]{0:T(1024)S(1)}, u32[]{:S(2)}) copy-start(s32[3072]{0:T(1024)S(1)} %fusion.77) | copy-start | bytes 36868
  279.7 89.5 %copy-start.3 = (bf16[256,1024]{1,0:T(8,128)(2,1)S(1)}, bf16[256,1024]{1,0:T(8,128)(2,1)}, u32[]{:S(2)}) copy-start(bf16[256,1024]{1,0:T(8,128)(2,1)} %param.16) | copy-start | bytes 1572868
  367.8 5.0 copy-start.16
  387.1 5.8 copy-start.21
  387.1 77.1 %all-to-all-start = ((bf16[8,4,96,1024]{3,2,1,0:T(8,128)(2,1)}), bf16[8,4,96,1024]{3,2,1,0:T(8,128)(2,1)}, u32[]{:S(2)}, u32[]{:S(2)}) async-start(bf16[8,4,96,1024]{3,2,1,0:T(8,128)(2,1)} %bitcast.146), calls=%async_computation | async-start | bytes 12582912 | tf_op jit(solution)/shard_map/all_to_all | solution.py:205
  393.0 4.2 copy-start.18
  393.0 4.2 slice-start.1
  393.0 4.6 copy-start.11
  464.2 18.2 %all-to-all-start.1 = ((bf16[8,4,96,64]{2,3,1,0:T(8,128)(2,1)}), bf16[8,4,96,64]{2,3,1,0:T(8,128)(2,1)S(1)}, u32[]{:S(2)}, u32[]{:S(2)}) async-start(bf16[8,4,96,64]{2,3,1,0:T(8,128)(2,1)} %copy.130), calls=%async_computation.1 | async-start | bytes 1048576 | tf_op jit(solution)/shard_map/all_to_all | solution.py:206
  491.2 1.7 copy-start.4
  494.8 14.8 %all-to-all-start.3 = ((bf16[8,4,96,32]{2,3,1,0:T(8,128)(2,1)}), bf16[8,4,96,32]{2,3,1,0:T(8,128)(2,1)S(1)}, u32[]{:S(2)}, u32[]{:S(2)}) async-start(bf16[8,4,96,32]{2,3,1,0:T(8,128)(2,1)} %fusion.45), calls=%async_computation.3 | async-start | bytes 524288 | tf_op jit(solution)/shard_map/all_to_all | solution.py:222
  509.5 5.4 copy-start.8
  509.5 5.6 copy-start.13
  509.5 5.8 copy-start.15
  509.5 5.8 copy-start.12
  509.6 76.4 %all-to-all-start.2 = ((bf16[8,4,96,1024]{3,2,1,0:T(8,128)(2,1)}), bf16[8,4,96,1024]{3,2,1,0:T(8,128)(2,1)}, u32[]{:S(2)}, u32[]{:S(2)}) async-start(bf16[8,4,96,1024]{3,2,1,0:T(8,128)(2,1)} %copy.134), calls=%async_computation.2 | async-start | bytes 12582912 | tf_op jit(solution)/shard_map/all_to_all | solution.py:221
  586.0 22.4 %copy-start.9 = (bf16[2,16,1024]{2,1,0:T(8,128)(2,1)S(1)}, bf16[2,16,1024]{2,1,0:T(8,128)(2,1)}, u32[]{:S(2)}) copy-start(bf16[2,16,1024]{2,1,0:T(8,128)(2,1)} %get-tuple-element.76) | copy-start | bytes 196612
  586.0 23.4 %copy-start.1 = (bf16[1024,1024]{1,0:T(8,128)(2,1)S(1)}, bf16[1024,1024]{1,0:T(8,128)(2,1)}, u32[]{:S(2)}) copy-start(bf16[1024,1024]{1,0:T(8,128)(2,1)} %param.22) | copy-start | bytes 6291460
Sparse Core Ops, SparseCore 0:
  9.5 73.6 all-gather.7
  85.3 70.3 all-gather.5
  170.5 55.2 all-gather.9
  227.8 51.8 all-gather.11
  281.7 46.8 all-gather.13
where the time goes:
time: 623 us; the launch traced here: 616 us
  waiting for transfers between devices  303 us (49%)
  local copies, waits for them, and re-layouts  110 us (18%)
  matrix products  107 us (17%)
  other arithmetic  60.4 us (10%)
  starting transfers between devices  20.4 us (3%)
  between operations  15.4 us (2%)
    all_gather x1, waiting for transfers between devices, per_device(): lax.all_gather(adapter_in, 'dp', axis=0, tiled=True)  67.7 us
    all_gather x1, waiting for transfers between devices, per_device(): lax.all_gather(adapter_out, 'dp', axis=0, tiled=True)  65.3 us
    all_to_all x1, waiting for transfers between devices, per_device(): lax.all_to_all(send_x, 'ep', split_axis=0, concat_axis=0, tiled=True)  56.4 us
    all_gather x1, waiting for transfers between devices, per_device(): vals_in = lax.all_gather(values_v, 'dp', axis=0, tiled=True)  53.9 us
    all_to_all x1, waiting for transfers between devices, per_device(): lax.all_to_all(expert_out, 'ep', split_axis=0, concat_axis=0, tiled=True)  45.3 us
    dot_general x1, matrix products, compute(): jnp.einsum('tgrs,sgd->tgrd', weights.astype(jnp.bfloat16), vals_in.reshap...  28.1 us
    dot_general x1, matrix products, compute(): jnp.einsum('tgrd,sgd->tgrs', query_grp, keys_in.reshape(rows_in, KV_HEADS...  26.5 us
    reduce_sum x1, other arithmetic, compute(): new_sum = jnp.sum(weights, axis=-1)  22.8 us
  transfers between devices with their start and end apart: 9, of which 6 were waited for; matrix products, arithmetic and copies ran while one was open for 37% of the time, Pallas kernels for 0%

commit v1 on v0

--- a/solution.py
+++ b/solution.py
@@ -11,6 +11,27 @@
 EPS = 1e-06
 THETA = 10000.0
 NEG_BIG = -1e30
+
+
+def gather_around(x, axis, dim):
+    size, here, rows = (lax.axis_size(axis), lax.axis_index(axis), x.shape[dim])
+    forward = [(i, (i + 1) % size) for i in range(size)]
+    downward = [(i, (i - 1) % size) for i in range(size)]
+    filled = jnp.zeros((*x.shape[:dim], size * rows, *x.shape[dim + 1 :]), x.dtype)
+    filled = lax.dynamic_update_slice_in_dim(filled, x, here * rows, axis=dim)
+    from_left = from_right = x
+    middle = size // 2
+    for step in range(1, middle + 1):
+        from_left = lax.ppermute(from_left, axis, forward)
+        filled = lax.dynamic_update_slice_in_dim(
+            filled, from_left, (here - step) % size * rows, axis=dim
+        )
+        if step < size - middle:
+            from_right = lax.ppermute(from_right, axis, downward)
+            filled = lax.dynamic_update_slice_in_dim(
+                filled, from_right, (here + step) % size * rows, axis=dim
+            )
+    return filled
 
 
 def rms_norm(values_in, gain_vec):
@@ -94,7 +115,7 @@
     position, req_start, slot_hot = request_layout(lengths[0], row_idx * tok_count, tok_count)
     group_ids = lax.dynamic_index_in_dim(adapter_ids, group_idx, 0, keepdims=False)
     all_in, all_out, all_expert = (
-        lax.all_gather(adapter_in, "dp", axis=0, tiled=True),
+        gather_around(adapter_in, "dp", 0),
         lax.all_gather(adapter_out, "dp", axis=0, tiled=True),
         lax.all_gather(adapter_expert, "dp", axis=0, tiled=True),
     )

time: 623 us -> 639 us (1.026)
  waiting for transfers between devices: 303 us -> 250 us
  starting transfers between devices: 20.4 us -> 55.9 us
  local copies, waits for them, and re-layouts: 110 us -> 139 us
    ppermute x0 -> x15, waiting for transfers between devices: none -> 81.3 us  [the longest x8 77.9 us: gather_around(): from_left = lax.ppermute(from_left, axis, forward)]
    all_gather x1 -> x0, waiting for transfers between devices: 67.7 us -> none  [per_device(): lax.all_gather(adapter_in, 'dp', axis=0, tiled=True)]
    all_gather x1, waiting for transfers between devices: 65.3 us -> 0.02 us  [per_device(): lax.all_gather(adapter_out, 'dp', axis=0, tiled=True)]
    ppermute x0 -> x15, starting transfers between devices: none -> 35.1 us  [the longest x7 32.9 us: gather_around(): from_right = lax.ppermute(from_right, axis, downward)]
    dynamic_update_slice x0 -> x16, local copies, waits for them, and re-layouts: none -> 24 us  [the longest x8 12 us: gather_around(): lax.dynamic_update_slice_in_dim(filled, from_left, (here - step) % size *...]
  transfers between devices with their start and end apart: 9 -> 23, of which waited for: 6 -> 13; matrix products, arithmetic and copies ran while one was open for 37% -> 41% of each run, Pallas kernels for 0% -> 0%
where the time goes in v1:
time: 639 us; the launch traced here: 628 us
  waiting for transfers between devices  250 us (39%)
  local copies, waits for them, and re-layouts  139 us (22%)
  matrix products  107 us (17%)
  other arithmetic  61.2 us (10%)
  starting transfers between devices  55.9 us (9%)
  between operations  15.5 us (2%)
    ppermute x8, waiting for transfers between devices, gather_around(): from_left = lax.ppermute(from_left, axis, forward)  77.9 us
    all_to_all x1, waiting for transfers between devices, per_device(): lax.all_to_all(send_x, 'ep', split_axis=0, concat_axis=0, tiled=True)  56.4 us
    all_gather x1, waiting for transfers between devices, per_device(): vals_in = lax.all_gather(values_v, 'dp', axis=0, tiled=True)  54 us
    all_to_all x1, waiting for transfers between devices, per_device(): lax.all_to_all(expert_out, 'ep', split_axis=0, concat_axis=0, tiled=True)  45.3 us
    ppermute x7, starting transfers between devices, gather_around(): from_right = lax.ppermute(from_right, axis, downward)  32.9 us
    dot_general x1, matrix products, compute(): jnp.einsum('tgrs,sgd->tgrd', weights.astype(jnp.bfloat16), vals_in.reshap...  28.1 us
    dot_general x1, matrix products, compute(): jnp.einsum('tgrd,sgd->tgrs', query_grp, keys_in.reshape(rows_in, KV_HEADS...  26.4 us
    reduce_sum x1, other arithmetic, compute(): new_sum = jnp.sum(weights, axis=-1)  22.8 us
  transfers between devices with their start and end apart: 23, of which 13 were waited for; matrix products, arithmetic and copies ran while one was open for 41% of the time, Pallas kernels for 0%

profile of v1, /device:TPU:1, one launch (start us, length us, event | category | flops | bytes accessed | tf_op | source)
XLA Modules:
  0.0 628.2 jit_solution(8081605480300294439)
XLA Ops:
  7.3 2.1 collective-permute-start
  9.4 3.8 collective-permute-start.1
  16.8 8.1 %collective-permute-done = bf16[4,1024,64]{1,2,0:T(8,128)(2,1)S(1)} collective-permute-done((bf16[4,1024,64]{1,2,0:T(8,128)(2,1)}, bf16[4,1024,64]{1,2,0:T(8,128)(2,1)S(1)}, u32[]{:S(2)}, u32[]{:S(2)}) %collective-permute-start) | collective-permute-done | bytes 524320 | tf_op jit(solution)/shard_map/ppermute | solution.py:25
  25.0 4.9 collective-permute-start.3
  30.6 17.7 %collective-permute-done.2 = bf16[4,1024,64]{1,2,0:T(8,128)(2,1)S(1)} collective-permute-done((bf16[4,1024,64]{1,2,0:T(8,128)(2,1)S(1)}, bf16[4,1024,64]{1,2,0:T(8,128)(2,1)S(1)}, u32[]{:S(2)}, u32[]{:S(2)}) %collective-permute-start.2) | collective-permute-done | bytes 524320 | tf_op jit(solution)/shard_map/ppermute | solution.py:25
  48.4 4.9 collective-permute-start.5
  53.3 13.5 %collective-permute-done.4 = bf16[4,1024,64]{1,2,0:T(8,128)(2,1)S(1)} collective-permute-done((bf16[4,1024,64]{1,2,0:T(8,128)(2,1)S(1)}, bf16[4,1024,64]{1,2,0:T(8,128)(2,1)S(1)}, u32[]{:S(2)}, u32[]{:S(2)}) %collective-permute-start.4) | collective-permute-done | bytes 524320 | tf_op jit(solution)/shard_map/ppermute | solution.py:25
  67.8 2.8 collective-permute-done.5
  70.6 5.5 collective-permute-start.7
  76.1 18.5 %collective-permute-done.6 = bf16[4,1024,64]{1,2,0:T(8,128)(2,1)S(1)} collective-permute-done((bf16[4,1024,64]{1,2,0:T(8,128)(2,1)S(1)}, bf16[4,1024,64]{1,2,0:T(8,128)(2,1)S(1)}, u32[]{:S(2)}, u32[]{:S(2)}) %collective-permute-start.6) | collective-permute-done | bytes 524320 | tf_op jit(solution)/shard_map/ppermute | solution.py:25
  94.7 5.2 fusion.72
  99.9 4.5 collective-permute-start.9
  104.5 4.3 broadcast_in_dim.167
  109.7 10.3 %collective-permute-done.8 = bf16[4,1024,64]{1,2,0:T(8,128)(2,1)} collective-permute-done((bf16[4,1024,64]{1,2,0:T(8,128)(2,1)S(1)}, bf16[4,1024,64]{1,2,0:T(8,128)(2,1)}, u32[]{:S(2)}, u32[]{:S(2)}) %collective-permute-start.8) | collective-permute-done | bytes 524320 | tf_op jit(solution)/shard_map/ppermute | solution.py:25
  124.9 4.6 collective-permute-start.11
  131.3 3.5 collective-permute-done.10
  142.4 4.8 collective-permute-start.13
  156.0 6.3 collective-permute-done.14
  163.1 3.9 gather_fusion
  167.9 3.9 gather_fusion.1
  172.7 3.9 convolution_add_fusion
  191.2 15.9 %reduce-window.11 = s32[32,16,128]{2,1,0:T(8,128)S(1)} reduce-window(s32[32,16,128]{2,1,0:T(8,128)} %fusion.69, s32[]{:T(128)} %constant.212.clone.1), window={size=1x1x128 pad=0_0x0_0x127_0}, to_apply=%region_11.12 | reduce-window | flops 8323072 | bytes 524292 | tf_op jit(solution)/shard_map/reduce-window.1
  212.9 8.2 %scatter_custom_fusion = s32[3072]{0:T(1024)S(1)} fusion(s32[2048]{0:T(1024)S(1)} %bitcast.173, s32[2048]{0:T(1024)} %add_select_fusion, s32[]{:T(128)} %constant.210.clone.1), kind=kCustom, calls=%fused_computation.129 | custom fusion | bytes 12800 | tf_op jit(solution)/shard_map/scatter | solution.py:219
  225.5 12.1 %all-gather.7.cloned.1.call-done = bf16[4096,512]{0,1:T(8,128)(2,1)} async-done(((bf16[256,512]{0,1:T(8,128)(2,1)}), bf16[4096,512]{0,1:T(8,128)(2,1)}) %all-gather.7.cloned.1.call-update) | async-done | bytes 4194320 | tf_op jit(solution)/shard_map/all_gather | solution.py:149
  237.6 54.0 %all-gather.9.cloned.1.call-done = bf16[4096,512]{1,0:T(8,128)(2,1)} async-done(((bf16[256,512]{1,0:T(8,128)(2,1)}), bf16[4096,512]{1,0:T(8,128)(2,1)}) %all-gather.9.cloned.1.call-update) | async-done | bytes 4194320 | tf_op jit(solution)/shard_map/all_gather | solution.py:150
  291.6 88.3 %conditional.1 = (f32[256,8,2]{0,2,1:T(2,128)S(1)}, f32[256,8,2,64]{0,3,2,1:T(8,128)}) conditional(s32[]{:T(128)} %bitcast.12, () %tuple.13, (s32[4096]{0:T(1024)S(1)}, s32[4096]{0:T(1024)S(1)}, s32[256]{0:T(256)}, s32[256]{0:T(256)}, bf16[4096,512]{0,1:T(8,128)(2,1)}, /*index=5*/bf16[256,8,2,64]{0,3,2,1:T(8,128)(2,1)S(1)}, ...), branch_computations={%region_4.5_spmd, %region_5.8_spmd} | conditional | flops 4516212736 | bytes 224004112 | solution.py:180
  291.6 4.6 compare_and_fusion
  296.2 26.4 %fusion = (f32[256,8,2]{0,2,1:T(2,128)S(1)}, f32[8,4096,256,2]{2,1,3,0:T(8,128)}) fusion(pred[256,4096]{0,1:T(8,128)(4,1)} %compare_and_fusion, bf16[4096,8,64,1]{0,2,3,1:T(8,128)(2,1)} %bitcast.176, bf16[256,8,2,64]{0,3,2,1:T(8,128)(2,1)S(1)} %get-tuple-element.23), kind=kOutput, calls=%fused_computation.11 | convolution fusion | flops 2197811200 | bytes 72892416 | tf_op jit(solution)/shard_map/cond/branch_1_fun/tgrd,sgd->tgrs/dot_general | solution.py:157
  322.7 22.8 %fusion.2 = f32[256,8,2]{0,2,1:T(2,128)S(1)} fusion(f32[8,4096,256,2]{2,1,3,0:T(8,128)} %get-tuple-element.65, f32[256,8,2]{0,2,1:T(2,128)S(1)} %broadcast_maximum_fusion, pred[256,4096]{0,1:T(8,128)(4,1)} %compare_and_fusion), kind=kLoop, calls=%fused_computation.13 | loop fusion | flops 83881984 | bytes 68190208 | tf_op jit(solution)/shard_map/cond/branch_1_fun/reduce_sum | solution.py:170
  345.5 6.4 %copy.117 = bf16[4096,512]{0,1:T(8,128)(2,1)} copy(bf16[4096,512]{1,0:T(8,128)(2,1)} %get-tuple-element.63) | data formatting | bytes 8388608 | tf_op jit(solution)/shard_map
  351.9 28.1 %fusion.6 = f32[256,8,2,64]{0,3,2,1:T(8,128)} fusion(bf16[4096,8,64,1]{0,2,3,1:T(8,128)(2,1)} %bitcast.150, f32[8,4096,256,2]{2,1,3,0:T(8,128)} %get-tuple-element.65, f32[256,8,2]{0,2,1:T(2,128)S(1)} %broadcast_maximum_fusion, pred[256,4096]{0,1:T(8,128)(4,1)} %compare_and_fusion), kind=kOutput, calls=%fused_computation.17 | convolution fusion | flops 2231369728 | bytes 73416704 | tf_op jit(solution)/shard_map/cond/branch_1_fun/tgrs,sgd->tgrd/dot_general | solution.py:171
  385.3 14.0 %gather_fusion.2 = bf16[3072,1024]{1,0:T(8,128)(2,1)} fusion(bf16[257,1024]{1,0:T(8,128)(2,1)S(1)} %concatenate.32, s32[3072]{0:T(1024)S(1)} %fusion.77), kind=kCustom, calls=%fused_computation.2 | custom fusion | bytes 12595200 | tf_op jit(solution)/shard_map/gather | solution.py:223
  399.3 5.9 all-to-all-start
  405.5 2.5 gather_fusion.4
  409.8 9.2 %gather_fusion.3 = bf16[3072,64]{1,0:T(8,128)(2,1)S(1)} fusion(bf16[257,64]{1,0:T(8,128)(2,1)S(1)} %concatenate.33.clone, s32[3072]{0:T(1024)S(1)} %copy-done.17), kind=kCustom, calls=%fused_computation.3 | custom fusion | bytes 798720 | tf_op jit(solution)/shard_map/gather | solution.py:224
  420.0 56.4 %all-to-all-done = bf16[8,4,96,1024]{3,2,1,0:T(8,128)(2,1)} async-done(((bf16[8,4,96,1024]{3,2,1,0:T(8,128)(2,1)}), bf16[8,4,96,1024]{3,2,1,0:T(8,128)(2,1)}, u32[]{:S(2)}, u32[]{:S(2)}) %all-to-all-start) | async-done | bytes 6291488 | tf_op jit(solution)/shard_map/all_to_all | solution.py:226
  476.3 4.4 all-to-all-start.1
  480.7 13.8 %fusion.12 = f32[4,8,96,1024]{3,2,1,0:T(8,128)} fusion(bf16[4,1024,1024]{2,1,0:T(8,128)(2,1)} %param.25, bf16[8,4,96,1024]{3,2,1,0:T(8,128)(2,1)} %all-to-all-done), kind=kOutput, calls=%fused_computation.23 | convolution fusion | flops 6442450944 | bytes 27262976 | tf_op jit(solution)/shard_map/jecd,edf->jecf/dot_general | solution.py:229
  494.5 6.7 %bitcast_add_fusion = f32[8,4,96,1024]{3,2,0,1:T(8,128)S(1)} fusion(f32[4,8,96,1024]{3,2,1,0:T(8,128)} %fusion.12, bf16[8,64,1024,1]{2,1,0,3:T(8,128)(2,1)} %bitcast.149, bf16[8,4,96,64]{2,3,1,0:T(8,128)(2,1)S(1)} %all-to-all-done.1), kind=kOutput, calls=%fused_computation.22 | convolution fusion | flops 405798912 | bytes 26607616 | tf_op jit(solution)/shard_map/jecr,jrf->jecf/dot_general | solution.py:230
  506.9 4.8 all-to-all-start.3
  511.7 6.6 %convert_bitcast_fusion = bf16[8,4,96,1024]{3,2,0,1:T(8,128)(2,1)S(1)} fusion(bf16[8,4,96,512]{3,2,0,1:T(8,128)(2,1)} %copy-done.4, bf16[4,512,1024]{2,1,0:T(8,128)(2,1)} %param.26), kind=kOutput, calls=%fused_computation.29 | convolution fusion | flops 3224371200 | bytes 13631488 | tf_op jit(solution)/shard_map/jech,ehd->jecd/dot_general | solution.py:234
  518.3 3.3 copy.134
  521.6 5.2 all-to-all-start.2
  527.7 16.8 %gather_fusion.7 = f32[2048]{0:T(1024)S(1)} fusion(f32[256,32]{0,1:T(8,128)S(1)} %fusion.100, s32[2048]{0:T(1024)S(1)} %reshape.451), kind=kCustom, calls=%fused_computation.7 | custom fusion | bytes 32768 | tf_op jit(solution)/shard_map/jit(take_along_axis)/gather | solution.py:194
  545.2 6.2 gather_fusion.6
  552.7 45.3 %all-to-all-done.2 = bf16[8,4,96,1024]{3,2,1,0:T(8,128)(2,1)} async-done(((bf16[8,4,96,1024]{3,2,1,0:T(8,128)(2,1)}), bf16[8,4,96,1024]{3,2,1,0:T(8,128)(2,1)}, u32[]{:S(2)}, u32[]{:S(2)}) %all-to-all-start.2) | async-done | bytes 6291488 | tf_op jit(solution)/shard_map/all_to_all | solution.py:242
  598.0 14.8 %gather_fusion.5 = bf16[2048,1024]{1,0:T(8,128)(2,1)} fusion(bf16[3072,1024]{1,0:T(8,128)(2,1)} %bitcast.48, s32[2048]{0:T(1024)S(1)} %broadcast_clamp_fusion), kind=kCustom, calls=%fused_computation.5 | custom fusion | bytes 8396800 | tf_op jit(solution)/shard_map/gather | solution.py:245
  612.9 7.5 %convert_reduce_fusion = f32[256,1024]{1,0:T(8,128)S(1)} fusion(bf16[2048,1024]{1,0:T(8,128)(2,1)} %gather_fusion.5, f32[256,8]{1,0:T(8,128)S(1)} %copy.121, s32[256,8]{1,0:T(8,128)S(1)} %copy.118), kind=kOutput, calls=%fused_computation.25 | convolution fusion | flops 207388672 | bytes 5259264 | tf_op jit(solution)/shard_map/tkg,tkd->tgd/dot_general | solution.py:255
  (192 shorter events, 73.6 us)
Async XLA Ops:
  6.5 374.8 %copy-start = (bf16[1024,1024]{1,0:T(8,128)(2,1)S(1)}, bf16[1024,1024]{1,0:T(8,128)(2,1)}, u32[]{:S(2)}) copy-start(bf16[1024,1024]{1,0:T(8,128)(2,1)} %param.22) | copy-start | bytes 6291460
  6.5 102.2 %copy-start.7 = (bf16[4,1024,64]{1,2,0:T(8,128)(2,1)S(1)}, bf16[4,1024,64]{1,2,0:T(8,128)(2,1)}, u32[]{:S(2)}) copy-start(bf16[4,1024,64]{1,2,0:T(8,128)(2,1)} %param.27) | copy-start | bytes 1572868
  6.5 161.4 %all-gather.5.cloned.1.call-start = ((), (), s32[]{:S(2)}) async-start(), calls=%async_computation.4 | async-start | bytes 8912896 | tf_op jit(solution)/shard_map/all_gather | solution.py:119
  7.3 230.3 %all-gather.7.cloned.1.call-start = ((), (), s32[]{:S(2)}) async-start(), calls=%async_computation.5 | async-start | bytes 4456448 | tf_op jit(solution)/shard_map/all_gather | solution.py:149
  7.3 17.6 %collective-permute-start = (bf16[4,1024,64]{1,2,0:T(8,128)(2,1)}, bf16[4,1024,64]{1,2,0:T(8,128)(2,1)S(1)}, u32[]{:S(2)}, u32[]{:S(2)}) collective-permute-start(bf16[4,1024,64]{1,2,0:T(8,128)(2,1)} %param.27), channel_id=1, source_target_pairs={{0,1},{1,2},{2,3},{3,4},{4,5},{5,6},{6,7},{7,8},{8,9},{9,10},{10,1... | collective-permute-start | bytes 1572872 | tf_op jit(solution)/shard_map/ppermute | solution.py:25
  9.4 15.6 %collective-permute-start.1 = (bf16[4,1024,64]{1,2,0:T(8,128)(2,1)}, bf16[4,1024,64]{1,2,0:T(8,128)(2,1)}, u32[]{:S(2)}, u32[]{:S(2)}) collective-permute-start(bf16[4,1024,64]{1,2,0:T(8,128)(2,1)} %param.27), channel_id=1, source_target_pairs={{0,15},{1,0},{2,1},{3,2},{4,3},{5,4},{6,5},{7,6},{8,7},{9,8},{10,9... | collective-permute-start | bytes 1572872 | tf_op jit(solution)/shard_map/ppermute | solution.py:30
  15.6 169.4 %copy-start.27 = (s32[256]{0:T(256)}, s32[256]{0:T(256)S(1)}, u32[]{:S(2)}) copy-start(s32[256]{0:T(256)S(1)} %iota_add_fusion) | copy-start | bytes 3076
  24.9 23.3 %collective-permute-start.2 = (bf16[4,1024,64]{1,2,0:T(8,128)(2,1)S(1)}, bf16[4,1024,64]{1,2,0:T(8,128)(2,1)S(1)}, u32[]{:S(2)}, u32[]{:S(2)}) collective-permute-start(bf16[4,1024,64]{1,2,0:T(8,128)(2,1)S(1)} %collective-permute-done), channel_id=1, source_target_pairs={{0,1},{1,2},{2,3},{3,4},{4,5},{5,6},{6,7},{7,8},{8,9},{9,10},{10,1... | collective-permute-start | bytes 1572872 | tf_op jit(solution)/shard_map/ppermute | solution.py:25
  25.0 147.7 %copy-start.23 = (pred[256,2]{0,1:T(4,128)(4,1)}, pred[256,2]{0,1:T(4,128)(4,1)S(1)}, u32[]{:S(2)}) copy-start(pred[256,2]{0,1:T(4,128)(4,1)S(1)} %iota_compare_fusion.7) | copy-start | bytes 1540
  25.0 23.3 %collective-permute-start.3 = (bf16[4,1024,64]{1,2,0:T(8,128)(2,1)}, bf16[4,1024,64]{1,2,0:T(8,128)(2,1)S(1)}, u32[]{:S(2)}, u32[]{:S(2)}) collective-permute-start(bf16[4,1024,64]{1,2,0:T(8,128)(2,1)} %collective-permute-done.1), channel_id=1, source_target_pairs={{0,15},{1,0},{2,1},{3,2},{4,3},{5,4},{6,5},{7,6},{8,7},{9,8},{10,9... | collective-permute-start | bytes 1572872 | tf_op jit(solution)/shard_map/ppermute | solution.py:30
  48.3 46.3 %copy-start.10 = (bf16[4,1024,64]{1,2,0:T(8,128)(2,1)}, bf16[4,1024,64]{1,2,0:T(8,128)(2,1)S(1)}, u32[]{:S(2)}) copy-start(bf16[4,1024,64]{1,2,0:T(8,128)(2,1)S(1)} %collective-permute-done.2) | copy-start | bytes 1572868
  48.3 18.5 %collective-permute-start.4 = (bf16[4,1024,64]{1,2,0:T(8,128)(2,1)S(1)}, bf16[4,1024,64]{1,2,0:T(8,128)(2,1)S(1)}, u32[]{:S(2)}, u32[]{:S(2)}) collective-permute-start(bf16[4,1024,64]{1,2,0:T(8,128)(2,1)S(1)} %collective-permute-done.2), channel_id=1, source_target_pairs={{0,1},{1,2},{2,3},{3,4},{4,5},{5,6},{6,7},{7,8},{8,9},{9,10},{10,1... | collective-permute-start | bytes 1572872 | tf_op jit(solution)/shard_map/ppermute | solution.py:25
  48.4 137.3 %copy-start.25 = (s32[256]{0:T(256)}, s32[256]{0:T(256)S(1)}, u32[]{:S(2)}) copy-start(s32[256]{0:T(256)S(1)} %select_reduce_fusion) | copy-start | bytes 3076
  48.4 46.2 %copy-start.9 = (bf16[4,1024,64]{1,2,0:T(8,128)(2,1)}, bf16[4,1024,64]{1,2,0:T(8,128)(2,1)S(1)}, u32[]{:S(2)}) copy-start(bf16[4,1024,64]{1,2,0:T(8,128)(2,1)S(1)} %collective-permute-done.3) | copy-start | bytes 1572868
  48.4 22.2 %collective-permute-start.5 = (bf16[4,1024,64]{1,2,0:T(8,128)(2,1)S(1)}, bf16[4,1024,64]{1,2,0:T(8,128)(2,1)S(1)}, u32[]{:S(2)}, u32[]{:S(2)}) collective-permute-start(bf16[4,1024,64]{1,2,0:T(8,128)(2,1)S(1)} %collective-permute-done.3), channel_id=1, source_target_pairs={{0,15},{1,0},{2,1},{3,2},{4,3},{5,4},{6,5},{7,6},{8,7},{9,8},{10,9... | collective-permute-start | bytes 1572872 | tf_op jit(solution)/shard_map/ppermute | solution.py:30
  67.6 27.0 %collective-permute-start.6 = (bf16[4,1024,64]{1,2,0:T(8,128)(2,1)S(1)}, bf16[4,1024,64]{1,2,0:T(8,128)(2,1)S(1)}, u32[]{:S(2)}, u32[]{:S(2)}) collective-permute-start(bf16[4,1024,64]{1,2,0:T(8,128)(2,1)S(1)} %collective-permute-done.4), channel_id=1, source_target_pairs={{0,1},{1,2},{2,3},{3,4},{4,5},{5,6},{6,7},{7,8},{8,9},{9,10},{10,1... | collective-permute-start | bytes 1572872 | tf_op jit(solution)/shard_map/ppermute | solution.py:25
  70.6 24.1 %copy-start.11 = (bf16[4,1024,64]{1,2,0:T(8,128)(2,1)}, bf16[4,1024,64]{1,2,0:T(8,128)(2,1)S(1)}, u32[]{:S(2)}) copy-start(bf16[4,1024,64]{1,2,0:T(8,128)(2,1)S(1)} %collective-permute-done.5) | copy-start | bytes 1572868
  70.6 29.4 %collective-permute-start.7 = (bf16[4,1024,64]{1,2,0:T(8,128)(2,1)S(1)}, bf16[4,1024,64]{1,2,0:T(8,128)(2,1)}, u32[]{:S(2)}, u32[]{:S(2)}) collective-permute-start(bf16[4,1024,64]{1,2,0:T(8,128)(2,1)S(1)} %collective-permute-done.5), channel_id=1, source_target_pairs={{0,15},{1,0},{2,1},{3,2},{4,3},{5,4},{6,5},{7,6},{8,7},{9,8},{10,9... | collective-permute-start | bytes 1572872 | tf_op jit(solution)/shard_map/ppermute | solution.py:30
  94.6 15.1 %copy-start.12 = (bf16[4,1024,64]{1,2,0:T(8,128)(2,1)}, bf16[4,1024,64]{1,2,0:T(8,128)(2,1)S(1)}, u32[]{:S(2)}) copy-start(bf16[4,1024,64]{1,2,0:T(8,128)(2,1)S(1)} %collective-permute-done.6) | copy-start | bytes 1572868
  94.6 25.3 %collective-permute-start.8 = (bf16[4,1024,64]{1,2,0:T(8,128)(2,1)S(1)}, bf16[4,1024,64]{1,2,0:T(8,128)(2,1)}, u32[]{:S(2)}, u32[]{:S(2)}) collective-permute-start(bf16[4,1024,64]{1,2,0:T(8,128)(2,1)S(1)} %collective-permute-done.6), channel_id=1, source_target_pairs={{0,1},{1,2},{2,3},{3,4},{4,5},{5,6},{6,7},{7,8},{8,9},{9,10},{10,1... | collective-permute-start | bytes 1572872 | tf_op jit(solution)/shard_map/ppermute | solution.py:25
  99.9 24.9 %collective-permute-start.9 = (bf16[4,1024,64]{1,2,0:T(8,128)(2,1)}, bf16[4,1024,64]{1,2,0:T(8,128)(2,1)}, u32[]{:S(2)}, u32[]{:S(2)}) collective-permute-start(bf16[4,1024,64]{1,2,0:T(8,128)(2,1)} %collective-permute-done.7), channel_id=1, source_target_pairs={{0,15},{1,0},{2,1},{3,2},{4,3},{5,4},{6,5},{7,6},{8,7},{9,8},{10,9... | collective-permute-start | bytes 1572872 | tf_op jit(solution)/shard_map/ppermute | solution.py:30
  120.0 14.9 %collective-permute-start.10 = (bf16[4,1024,64]{1,2,0:T(8,128)(2,1)}, bf16[4,1024,64]{1,2,0:T(8,128)(2,1)}, u32[]{:S(2)}, u32[]{:S(2)}) collective-permute-start(bf16[4,1024,64]{1,2,0:T(8,128)(2,1)} %collective-permute-done.8), channel_id=1, source_target_pairs={{0,1},{1,2},{2,3},{3,4},{4,5},{5,6},{6,7},{7,8},{8,9},{9,10},{10,1... | collective-permute-start | bytes 1572872 | tf_op jit(solution)/shard_map/ppermute | solution.py:25
  123.0 49.8 %copy-start.2 = (bf16[256,1024]{1,0:T(8,128)(2,1)S(1)}, bf16[256,1024]{1,0:T(8,128)(2,1)}, u32[]{:S(2)}) copy-start(bf16[256,1024]{1,0:T(8,128)(2,1)} %param.16) | copy-start | bytes 1572868
  124.9 17.5 %collective-permute-start.11 = (bf16[4,1024,64]{1,2,0:T(8,128)(2,1)}, bf16[4,1024,64]{1,2,0:T(8,128)(2,1)S(1)}, u32[]{:S(2)}, u32[]{:S(2)}) collective-permute-start(bf16[4,1024,64]{1,2,0:T(8,128)(2,1)} %collective-permute-done.9), channel_id=1, source_target_pairs={{0,15},{1,0},{2,1},{3,2},{4,3},{5,4},{6,5},{7,6},{8,7},{9,8},{10,9... | collective-permute-start | bytes 1572872 | tf_op jit(solution)/shard_map/ppermute | solution.py:30
  134.8 14.3 %collective-permute-start.12 = (bf16[4,1024,64]{1,2,0:T(8,128)(2,1)}, bf16[4,1024,64]{1,2,0:T(8,128)(2,1)S(1)}, u32[]{:S(2)}, u32[]{:S(2)}) collective-permute-start(bf16[4,1024,64]{1,2,0:T(8,128)(2,1)} %collective-permute-done.10), channel_id=1, source_target_pairs={{0,1},{1,2},{2,3},{3,4},{4,5},{5,6},{6,7},{7,8},{8,9},{9,10},{10,1... | collective-permute-start | bytes 1572872 | tf_op jit(solution)/shard_map/ppermute | solution.py:25
  142.4 12.7 %collective-permute-start.13 = (bf16[4,1024,64]{1,2,0:T(8,128)(2,1)S(1)}, bf16[4,1024,64]{1,2,0:T(8,128)(2,1)S(1)}, u32[]{:S(2)}, u32[]{:S(2)}) collective-permute-start(bf16[4,1024,64]{1,2,0:T(8,128)(2,1)S(1)} %collective-permute-done.11), channel_id=1, source_target_pairs={{0,15},{1,0},{2,1},{3,2},{4,3},{5,4},{6,5},{7,6},{8,7},{9,8},{10,9... | collective-permute-start | bytes 1572872 | tf_op jit(solution)/shard_map/ppermute | solution.py:30
  149.1 13.1 %collective-permute-start.14 = (bf16[4,1024,64]{1,2,0:T(8,128)(2,1)S(1)}, bf16[4,1024,64]{1,2,0:T(8,128)(2,1)S(1)}, u32[]{:S(2)}, u32[]{:S(2)}) collective-permute-start(bf16[4,1024,64]{1,2,0:T(8,128)(2,1)S(1)} %collective-permute-done.12), channel_id=1, source_target_pairs={{0,1},{1,2},{2,3},{3,4},{4,5},{5,6},{6,7},{7,8},{8,9},{9,10},{10,1... | collective-permute-start | bytes 1572872 | tf_op jit(solution)/shard_map/ppermute | solution.py:25
  152.8 33.3 %copy-start.13 = (s32[256,8]{0,1:T(8,128)S(1)}, s32[256,8]{0,1:T(8,128)}, u32[]{:S(2)}) copy-start(s32[256,8]{0,1:T(8,128)} %param.19) | copy-start | bytes 24580
  153.7 35.3 %copy-start.28 = (bf16[1024]{0:T(1024)(128)(2,1)S(1)}, bf16[1024]{0:T(1024)(128)(2,1)}, u32[]{:S(2)}) copy-start(bf16[1024]{0:T(1024)(128)(2,1)} %param.23) | copy-start | bytes 6148
  176.7 46.0 %slice-start = ((f32[256,2048]{1,0:T(8,128)}), f32[256,1024]{1,0:T(8,128)S(1)}, s32[]{:S(2)}) async-start(f32[256,2048]{1,0:T(8,128)} %convolution_add_fusion), calls=%async_computation.8 | async-start | bytes 2097152 | tf_op jit(solution)/shard_map/slice | solution.py:131
  182.5 109.1 %all-gather.9.cloned.1.call-start = ((), (), s32[]{:S(2)}) async-start(), calls=%async_computation.6 | async-start | bytes 4456448 | tf_op jit(solution)/shard_map/all_gather | solution.py:150
  184.4 221.0 %all-gather.11.cloned.1.call-start = ((), (), s32[]{:S(2)}) async-start(), calls=%async_computation.7 | async-start | bytes 3342336 | tf_op jit(solution)/shard_map/all_gather | solution.py:120
  212.9 8.2 %copy-start.20 = (s32[2048,1]{0,1:T(1,128)}, s32[2048,1]{0,1:T(1,128)S(1)}, u32[]{:S(2)}) copy-start(s32[2048,1]{0,1:T(1,128)S(1)} %compare_select_fusion) | copy-start | bytes 24580
  221.1 164.1 %copy-start.16 = (s32[3072]{0:T(1024)}, s32[3072]{0:T(1024)S(1)}, u32[]{:S(2)}) copy-start(s32[3072]{0:T(1024)S(1)} %fusion.77) | copy-start | bytes 36868
  291.6 89.7 %copy-start.3 = (bf16[256,1024]{1,0:T(8,128)(2,1)S(1)}, bf16[256,1024]{1,0:T(8,128)(2,1)}, u32[]{:S(2)}) copy-start(bf16[256,1024]{1,0:T(8,128)(2,1)} %param.16) | copy-start | bytes 1572868
  291.6 93.4 %copy-start.22 = (f32[1024]{0:T(1024)S(1)}, f32[1024]{0:T(1024)}, u32[]{:S(2)}) copy-start(f32[1024]{0:T(1024)} %convert_element_type.120) | copy-start | bytes 12292
  399.3 5.9 copy-start.26
  399.3 10.0 %copy-start.24 = (pred[256,2]{0,1:T(4,128)(4,1)S(1)}, pred[256,2]{0,1:T(4,128)(4,1)}, u32[]{:S(2)}) copy-start(pred[256,2]{0,1:T(4,128)(4,1)} %copy-done.23) | copy-start | bytes 1540
  399.3 10.0 %slice-start.1 = ((bf16[2,1024,64]{1,2,0:T(8,128)(2,1)}), bf16[2,1024,32]{1,2,0:T(8,128)(2,1)S(1)}, s32[]{:S(2)}) async-start(bf16[2,1024,64]{1,2,0:T(8,128)(2,1)} %copy-done.5), calls=%async_computation.9 | async-start | bytes 262144 | tf_op jit(solution)/shard_map/slice | solution.py:195
  399.3 10.5 %copy-start.17 = (s32[3072]{0:T(1024)S(1)}, s32[3072]{0:T(1024)}, u32[]{:S(2)}) copy-start(s32[3072]{0:T(1024)} %copy-done.16) | copy-start | bytes 36868
  399.3 77.1 %all-to-all-start = ((bf16[8,4,96,1024]{3,2,1,0:T(8,128)(2,1)}), bf16[8,4,96,1024]{3,2,1,0:T(8,128)(2,1)}, u32[]{:S(2)}, u32[]{:S(2)}) async-start(bf16[8,4,96,1024]{3,2,1,0:T(8,128)(2,1)} %bitcast.146), calls=%async_computation | async-start | bytes 12582912 | tf_op jit(solution)/shard_map/all_to_all | solution.py:226
  476.3 18.2 %all-to-all-start.1 = ((bf16[8,4,96,64]{2,3,1,0:T(8,128)(2,1)}), bf16[8,4,96,64]{2,3,1,0:T(8,128)(2,1)S(1)}, u32[]{:S(2)}, u32[]{:S(2)}) async-start(bf16[8,4,96,64]{2,3,1,0:T(8,128)(2,1)} %copy.130), calls=%async_computation.1 | async-start | bytes 1048576 | tf_op jit(solution)/shard_map/all_to_all | solution.py:227
  506.9 14.8 %all-to-all-start.3 = ((bf16[8,4,96,32]{2,3,1,0:T(8,128)(2,1)}), bf16[8,4,96,32]{2,3,1,0:T(8,128)(2,1)S(1)}, u32[]{:S(2)}, u32[]{:S(2)}) async-start(bf16[8,4,96,32]{2,3,1,0:T(8,128)(2,1)} %fusion.45), calls=%async_computation.3 | async-start | bytes 524288 | tf_op jit(solution)/shard_map/all_to_all | solution.py:243
  521.6 5.8 copy-start.21
  521.6 5.8 copy-start.18
  521.6 76.4 %all-to-all-start.2 = ((bf16[8,4,96,1024]{3,2,1,0:T(8,128)(2,1)}), bf16[8,4,96,1024]{3,2,1,0:T(8,128)(2,1)}, u32[]{:S(2)}, u32[]{:S(2)}) async-start(bf16[8,4,96,1024]{3,2,1,0:T(8,128)(2,1)} %copy.134), calls=%async_computation.2 | async-start | bytes 12582912 | tf_op jit(solution)/shard_map/all_to_all | solution.py:242
  598.0 22.4 %copy-start.15 = (bf16[2,16,1024]{2,1,0:T(8,128)(2,1)S(1)}, bf16[2,16,1024]{2,1,0:T(8,128)(2,1)}, u32[]{:S(2)}) copy-start(bf16[2,16,1024]{2,1,0:T(8,128)(2,1)} %get-tuple-element.76) | copy-start | bytes 196612
  598.0 23.4 %copy-start.1 = (bf16[1024,1024]{1,0:T(8,128)(2,1)S(1)}, bf16[1024,1024]{1,0:T(8,128)(2,1)}, u32[]{:S(2)}) copy-start(bf16[1024,1024]{1,0:T(8,128)(2,1)} %param.22) | copy-start | bytes 6291460
  (6 other events, 14.9 us)
Sparse Core Ops, SparseCore 0:
  9.5 109.1 all-gather.4
  182.7 54.8 all-gather.6
  239.7 51.8 all-gather.8
  293.6 46.8 all-gather.10
